TPU v7x, 128 devices: a whole 4x4x4 slice. The times are simulated.
128 devices in a mesh: mem: 2 (over core), state: 64 (over y, x, z).
Axes of the slice: x: 4, y: 4, z: 4, core: 2. Of those that a mesh axis runs over, the one named last changes fastest.
Arguments:
- background_ensemble: bfloat16 [80, 4194304], P('mem', 'state'), may hold values from -6 to 6
- measured_segment_index: int32 [2, 256], replicated, may hold values from 0 to 127
- measured_place_within_segment: int32 [2, 256], replicated, may hold values from 0 to 32767
- measured_readings: float32 [2, 256], replicated, may hold values from -6 to 6
- measured_noise_spread: float32 [2, 256], replicated, may hold values from 0.25 to 4
- measured_damping_weight: float32 [2, 256], replicated, may hold values from 0.3 to 1
- measured_cutoff_extent: int32 [2, 256], replicated, may hold values from 1 to 1024
Outputs:
- analysis: bfloat16 [80, 4194304], P('mem', 'state')
Inputs may be any that keep to these rules, and one draw needn't show every extreme that they name: measured_segment_index numbers the blocks of 32768 state values in the order of the state dimension. measured_place_within_segment is a position inside the owner's block.
All inputs are finite; a program needn't handle non-finite values.
Results may differ from a plain program's by a relative error of at most 0.0051.
Values may be sent and summed in bfloat16 or wider, within the bound.
No kernel may reach another device: no remote copies, remote signals or barrier semaphores. Data moves between devices by JAX's collectives and lax.ppermute only.
A program may use at most 64 MiB of HBM per device.

v0:
```python
import jax
import jax.numpy as jnp
from jax import lax
from jax.sharding import Mesh
from jax.sharding import PartitionSpec as P

ENSEMBLE_COUNT = 80
SD = 32768
B = 2
LB = 128
BLK = 4096
STATE = ("state_0", "state_1", "state_2")


def split_up(array, dim, size):
    dims = array.shape
    blocks = array.reshape(*dims[:dim], size, dims[dim] // size, *dims[dim + 1 :])
    return jnp.moveaxis(blocks, dim, 0)


def sum_at_owner(array, axis, dim):
    blocks = split_up(array, dim, lax.axis_size(axis))
    arrived = lax.all_to_all(blocks, axis, split_axis=0, concat_axis=0, tiled=True)
    return arrived.sum(axis=0)


def summed_rows(array, axes, dim):
    far, near = axes
    own = sum_at_owner(split_up(array, dim, lax.axis_size(far)), near, dim + 1)
    return jnp.sum(lax.all_to_all(own, far, 0, 0, tiled=True), axis=0)


def filled_up(lines, size):
    spare = -lines.shape[0] % size
    if not spare:
        return lines
    return jnp.concatenate([lines, jnp.zeros((spare, *lines.shape[1:]), lines.dtype)])


def sent_to_all(array, axis):
    size = lax.axis_size(axis)
    return lax.all_to_all(
        jnp.broadcast_to(array[None], (size, *array.shape)), axis, 0, 0, tiled=True
    )


def joined_along(blocks, dim):
    blocks = jnp.moveaxis(blocks, 0, dim)
    dims = blocks.shape
    return blocks.reshape(*dims[:dim], dims[dim] * dims[dim + 1], *dims[dim + 2 :])


def gather_axes(array, axes, dim):
    far, near = axes
    blocks = sent_to_all(sent_to_all(array, far), near)
    return joined_along(blocks.swapaxes(0, 1).reshape(-1, *array.shape), dim)


def total_of(array, axes):
    lines = array.reshape(-1)
    own = summed_rows(filled_up(lines, lax.axis_size(axes[0]) * lax.axis_size(axes[1])), axes, 0)
    whole = gather_axes(own, axes, 0)
    return whole[: len(lines)].reshape(array.shape)


def observe_stats(prior_ens, values, variances):
    centre = jnp.mean(prior_ens, axis=0)
    anomaly = prior_ens - centre
    prior_var = jnp.sum(anomaly * anomaly, axis=0) / (ENSEMBLE_COUNT - 1) + 1e-06
    post_var = 1.0 / (1.0 / prior_var + 1.0 / variances)
    post_mean = post_var * (centre / prior_var + values / variances)
    shrink = jnp.sqrt(post_var / prior_var)
    increment = (post_mean - centre + (shrink - 1.0) * anomaly).astype(jnp.bfloat16)
    scaling = 1.0 / ((ENSEMBLE_COUNT - 1) * prior_var)
    return (increment, anomaly.astype(jnp.bfloat16), scaling)


def taper_weights(columns, obs_index, taper_row, reach_row):
    distance = jnp.abs(columns[:, None] // LB - obs_index[None, :] // LB).astype(jnp.float32)
    return taper_row[None, :] * jnp.maximum(
        0.0, 1.0 - distance / (reach_row[None, :].astype(jnp.float32) + 1.0)
    )


def update_block(
    block_values, columns, obs_index, taper_row, reach_row, increment, anomaly, scaling
):
    values = block_values.astype(jnp.float32)
    centred = (values - jnp.mean(values, axis=0)).astype(jnp.bfloat16)
    covariance = lax.dot_general(
        centred, anomaly, (((0,), (0,)), ((), ())), preferred_element_type=jnp.float32
    )
    gain_matrix = (
        taper_weights(columns, obs_index, taper_row, reach_row) * covariance * scaling[None, :]
    ).astype(jnp.bfloat16)
    change = lax.dot_general(
        increment, gain_matrix, (((1,), (1,)), ((), ())), preferred_element_type=jnp.float32
    )
    return (values + change).astype(jnp.bfloat16)


def collect_prior(realization_vectors, owner_row, local_row, my_block, col_offset):
    picked = jnp.take(realization_vectors, col_offset + local_row, axis=1).astype(jnp.float32)
    return jnp.where((owner_row == my_block)[None, :], picked, 0.0)


def apply_batch(
    realization_vectors, column_base, obs_index, taper_row, reach_row, increment, anomaly, scaling
):

    def advance(block_no, buffer):
        start_col = block_no * BLK
        block_values = lax.dynamic_slice_in_dim(buffer, start_col, BLK, 1)
        columns = column_base + start_col + jnp.arange(BLK, dtype=jnp.int32)
        renewed = update_block(
            block_values, columns, obs_index, taper_row, reach_row, increment, anomaly, scaling
        )
        return lax.dynamic_update_slice_in_dim(buffer, renewed, start_col, 1)

    return lax.fori_loop(0, realization_vectors.shape[1] // BLK, advance, realization_vectors)


def on_device(
    background_ensemble,
    measured_segment_index,
    measured_place_within_segment,
    measured_readings,
    measured_noise_spread,
    measured_damping_weight,
    measured_cutoff_extent,
):
    pieces = lax.axis_size("mem")
    member_row = lax.axis_index("mem")
    slab_index = lax.axis_index(STATE)
    my_block = slab_index * pieces + member_row
    realization_vectors = lax.all_to_all(
        background_ensemble, "mem", split_axis=1, concat_axis=0, tiled=True
    )
    column_base = my_block * SD
    col_offset = 0
    for batch_no in range(B):
        if batch_no == 0:
            prior_ens = total_of(
                collect_prior(
                    realization_vectors,
                    measured_segment_index[0],
                    measured_place_within_segment[0],
                    my_block,
                    col_offset,
                ),
                ("mem", ("state_0", "state_1", "state_2")),
            )
        else:
            prior_ens = total_of(
                collect_prior(
                    realization_vectors,
                    measured_segment_index[batch_no],
                    measured_place_within_segment[batch_no],
                    my_block,
                    col_offset,
                ),
                ("mem", ("state_0", "state_1", "state_2")),
            )
        obs_index = measured_segment_index[batch_no] * SD + measured_place_within_segment[batch_no]
        increment, anomaly, scaling = observe_stats(
            prior_ens, measured_readings[batch_no], measured_noise_spread[batch_no]
        )
        realization_vectors = apply_batch(
            realization_vectors,
            column_base,
            obs_index,
            measured_damping_weight[batch_no],
            measured_cutoff_extent[batch_no],
            increment,
            anomaly,
            scaling,
        )
    return lax.all_to_all(realization_vectors, "mem", split_axis=0, concat_axis=1, tiled=True)


def solution(mesh):
    torus = Mesh(
        mesh.devices.reshape(mesh.shape["mem"], 4, 4, 4), ("mem", "state_0", "state_1", "state_2")
    )
    in_specs = (P("mem", STATE), P(), P(), P(), P(), P(), P())
    out_specs = P("mem", STATE)
    return jax.shard_map(
        on_device, mesh=torus, in_specs=in_specs, out_specs=out_specs, check_vma=False
    )
```

profile of v0, /device:TPU:1, one launch (start us, length us, event | category | flops | bytes accessed | tf_op | source)
XLA Modules:
  0.0 211.1 jit_solution(6932354710521923166)
XLA Ops:
  0.0 5.2 %copy.47 = bf16[5,2,8,32768]{3,2,0,1:T(8,128)(2,1)} copy(bf16[5,2,8,32768]{3,2,1,0:T(8,128)(2,1)} %bitcast.89) | data formatting | bytes 10485760 | tf_op jit(solution)/shard_map/all_to_all | solution.py:136
  5.2 7.5 %all-to-all-start = ((bf16[40,2,32768]{2,0,1:T(8,128)(2,1)}), bf16[40,2,32768]{2,0,1:T(8,128)(2,1)}, u32[]{:S(2)}, u32[]{:S(2)}) async-start(bf16[40,2,32768]{2,0,1:T(8,128)(2,1)} %bitcast.87), calls=%async_computation | async-start | bytes 10485760 | tf_op jit(solution)/shard_map/all_to_all | solution.py:136
  12.8 4.8 %all-to-all-done = bf16[40,2,32768]{2,0,1:T(8,128)(2,1)} async-done(((bf16[40,2,32768]{2,0,1:T(8,128)(2,1)}), bf16[40,2,32768]{2,0,1:T(8,128)(2,1)}, u32[]{:S(2)}, u32[]{:S(2)}) %all-to-all-start) | async-done | bytes 5242912 | tf_op jit(solution)/shard_map/all_to_all | solution.py:136
  17.6 9.5 %copy.31 = bf16[80,32768]{0,1:T(8,128)(2,1)} copy(bf16[80,32768]{1,0:T(8,128)(2,1)} %bitcast.9) | data formatting | bytes 10485760 | tf_op jit(solution)/shard_map/all_to_all | solution.py:136
  27.2 5.2 %gather_fusion = bf16[256,80]{1,0:T(8,128)(2,1)S(1)} fusion(bf16[80,32768]{0,1:T(8,128)(2,1)} %copy.31, s32[1024]{0:T(1024)S(1)} %pad_clamp_fusion.1), kind=kCustom, calls=%fused_computation.clone | custom fusion | bytes 82944 | tf_op jit(solution)/shard_map/jit(_take)/gather | solution.py:103
  33.4 11.2 %all-to-all-start.1 = ((f32[64,2,160]{2,1,0:T(2,128)}), f32[64,2,160]{2,1,0:T(2,128)S(1)}, u32[]{:S(2)}, u32[]{:S(2)}) async-start(f32[64,2,160]{2,1,0:T(2,128)} %copy.33), calls=%async_computation.1 | async-start | bytes 262144 | tf_op jit(solution)/shard_map/all_to_all | solution.py:23
  44.7 8.7 %all-to-all-done.1 = f32[64,2,160]{2,1,0:T(2,128)S(1)} async-done(((f32[64,2,160]{2,1,0:T(2,128)}), f32[64,2,160]{2,1,0:T(2,128)S(1)}, u32[]{:S(2)}, u32[]{:S(2)}) %all-to-all-start.1) | async-done | bytes 81952 | tf_op jit(solution)/shard_map/all_to_all | solution.py:23
  53.5 5.2 %all_to_all.88 = f32[2,1,160]{2,1,0:T(1,128)S(1)} all-to-all(f32[2,1,160]{2,1,0:T(1,128)S(1)} %all_to_all.65), channel_id=1, replica_groups=mesh['mem'=2,'state_0'=4,'state_1'=4,'state_2'=4] {'mem'}, dimensions={0} | all-to-all | bytes 2560 | tf_op jit(solution)/shard_map/all_to_all | solution.py:30
  58.7 3.7 %all_to_all.89 = f32[2,1,160]{2,1,0:T(1,128)S(1)} all-to-all(f32[2,1,160]{2,1,0:T(1,128)S(1)} %broadcast_in_dim.94), channel_id=1, replica_groups=mesh['mem'=2,'state_0'=4,'state_1'=4,'state_2'=4] {'mem'}, dimensions={0} | all-to-all | bytes 2560 | tf_op jit(solution)/shard_map/all_to_all | solution.py:42
  63.1 4.7 %all-to-all-start.4 = ((f32[64,2,160]{2,1,0:T(2,128)}), f32[64,2,160]{2,1,0:T(2,128)S(1)}, u32[]{:S(2)}, u32[]{:S(2)}) async-start(f32[64,2,160]{2,1,0:T(2,128)} %broadcast_in_dim.96), calls=%async_computation.4 | async-start | bytes 262144 | tf_op jit(solution)/shard_map/all_to_all | solution.py:42
  67.8 8.7 %all-to-all-done.4 = f32[64,2,160]{2,1,0:T(2,128)S(1)} async-done(((f32[64,2,160]{2,1,0:T(2,128)}), f32[64,2,160]{2,1,0:T(2,128)S(1)}, u32[]{:S(2)}, u32[]{:S(2)}) %all-to-all-start.4) | async-done | bytes 81952 | tf_op jit(solution)/shard_map/all_to_all | solution.py:42
  76.9 33.8 %while.32 = (s32[]{:T(128)}, bf16[80,32768]{1,0:T(8,128)(2,1)}, f32[1,256]{1,0:T(1,128)S(1)}, s32[]{:T(128)}, s32[1,256]{1,0:T(1,128)S(1)}, /*index=5*/s32[256]{...) while((s32[]{:T(128)}, bf16[80,32768]{1,0:T(8,128)(2,1)}, ...), condition=%wide.region_6.8_spmd, body=%wide.region_4.7_spmd.sunk | while | flops 348720640 | bytes 3467987 | solution.py:120
  90.9 2.9 %fusion.48 = bf16[80,32768]{1,0:T(8,128)(2,1)} fusion(bf16[80,32768]{1,0:T(8,128)(2,1)} %get-tuple-element.801, s32[]{:T(128)S(6)} %select_n.138, bf16[80,256]{1,0:T(8,128)(2,1)S(1)} %get-tuple-element.825, bf16[80,4096]{1,0:T(8,128)(2,1)S(1)} %get-tuple-element.770, bf16[80,256]{1,0:T(8,128)(2,1)S(1)} %get-tuple-element.823, ...), kind=kOutput, calls=%fused_computation.8.clone.1 | convolution fusion | flops 347996160 | bytes 2084868 | tf_op jit(solution)/shard_map/while/body/eval_jaxpr/dot_general | solution.py:96
  110.6 9.5 %copy.35 = bf16[80,32768]{0,1:T(8,128)(2,1)} copy(bf16[80,32768]{1,0:T(8,128)(2,1)} %get-tuple-element.831) | data formatting | bytes 10485760 | tf_op jit(solution)/shard_map/while | solution.py:120
  120.1 5.2 %gather_fusion.1 = bf16[256,80]{1,0:T(8,128)(2,1)S(1)} fusion(bf16[80,32768]{0,1:T(8,128)(2,1)} %copy.35, s32[1024]{0:T(1024)S(1)} %pad_clamp_fusion), kind=kCustom, calls=%fused_computation.1.clone | custom fusion | bytes 82944 | tf_op jit(solution)/shard_map/jit(_take)/gather | solution.py:103
  125.8 13.5 %all_to_all.90 = f32[64,2,160]{2,1,0:T(2,128)S(1)} all-to-all(f32[64,2,160]{2,1,0:T(2,128)S(1)} %copy.37), channel_id=1, replica_groups=mesh['mem'=2,'state_0'=4,'state_1'=4,'state_2'=4] {'state_0','state_1','..., dimensions={0} | all-to-all | bytes 163840 | tf_op jit(solution)/shard_map/all_to_all | solution.py:23
  139.4 6.2 %all_to_all.91 = f32[2,1,160]{2,1,0:T(1,128)S(1)} all-to-all(f32[2,1,160]{2,1,0:T(1,128)S(1)} %all_to_all.70), channel_id=1, replica_groups=mesh['mem'=2,'state_0'=4,'state_1'=4,'state_2'=4] {'mem'}, dimensions={0} | all-to-all | bytes 2560 | tf_op jit(solution)/shard_map/all_to_all | solution.py:30
  145.7 3.7 %all_to_all.92 = f32[2,1,160]{2,1,0:T(1,128)S(1)} all-to-all(f32[2,1,160]{2,1,0:T(1,128)S(1)} %broadcast_in_dim.99), channel_id=1, replica_groups=mesh['mem'=2,'state_0'=4,'state_1'=4,'state_2'=4] {'mem'}, dimensions={0} | all-to-all | bytes 2560 | tf_op jit(solution)/shard_map/all_to_all | solution.py:42
  150.1 4.9 %all-to-all-start.8 = ((f32[64,2,160]{2,1,0:T(2,128)}), f32[64,2,160]{2,1,0:T(2,128)S(1)}, u32[]{:S(2)}, u32[]{:S(2)}) async-start(f32[64,2,160]{2,1,0:T(2,128)} %broadcast_in_dim.101), calls=%async_computation.8 | async-start | bytes 262144 | tf_op jit(solution)/shard_map/all_to_all | solution.py:42
  154.9 8.6 %all-to-all-done.8 = f32[64,2,160]{2,1,0:T(2,128)S(1)} async-done(((f32[64,2,160]{2,1,0:T(2,128)}), f32[64,2,160]{2,1,0:T(2,128)S(1)}, u32[]{:S(2)}, u32[]{:S(2)}) %all-to-all-start.8) | async-done | bytes 81952 | tf_op jit(solution)/shard_map/all_to_all | solution.py:42
  163.8 33.8 %while.33 = (s32[]{:T(128)}, bf16[80,32768]{1,0:T(8,128)(2,1)}, f32[1,256]{1,0:T(1,128)S(1)}, s32[]{:T(128)}, s32[1,256]{1,0:T(1,128)S(1)}, /*index=5*/s32[256]{...) while((s32[]{:T(128)}, bf16[80,32768]{1,0:T(8,128)(2,1)}, ...), condition=%wide.region_13.15_spmd, body=%wide.region_11.14_spmd.sunk | while | flops 348720640 | bytes 3467987 | solution.py:120
  177.8 3.0 %fusion.52 = bf16[80,32768]{1,0:T(8,128)(2,1)} fusion(bf16[80,32768]{1,0:T(8,128)(2,1)} %get-tuple-element.846, s32[]{:T(128)S(6)} %select_n.141, bf16[80,256]{1,0:T(8,128)(2,1)S(1)} %get-tuple-element.870, bf16[80,4096]{1,0:T(8,128)(2,1)S(1)} %get-tuple-element.783, bf16[80,256]{1,0:T(8,128)(2,1)S(1)} %get-tuple-element.868, ...), kind=kOutput, calls=%fused_computation.38.clone.1 | convolution fusion | flops 347996160 | bytes 2084868 | tf_op jit(solution)/shard_map/while/body/eval_jaxpr/dot_general | solution.py:96
  194.7 2.9 %fusion.52 = bf16[80,32768]{1,0:T(8,128)(2,1)} fusion(bf16[80,32768]{1,0:T(8,128)(2,1)} %get-tuple-element.846, s32[]{:T(128)S(6)} %select_n.141, bf16[80,256]{1,0:T(8,128)(2,1)S(1)} %get-tuple-element.870, bf16[80,4096]{1,0:T(8,128)(2,1)S(1)} %get-tuple-element.783, bf16[80,256]{1,0:T(8,128)(2,1)S(1)} %get-tuple-element.868, ...), kind=kOutput, calls=%fused_computation.38.clone.1 | convolution fusion | flops 347996160 | bytes 2084868 | tf_op jit(solution)/shard_map/while/body/eval_jaxpr/dot_general | solution.py:96
  197.6 10.8 %all_to_all.93 = bf16[2,40,32768]{2,1,0:T(8,128)(2,1)S(1)} all-to-all(bf16[2,40,32768]{2,1,0:T(8,128)(2,1)} %bitcast.29), channel_id=1, replica_groups=mesh['mem'=2,'state_0'=4,'state_1'=4,'state_2'=4] {'mem'}, dimensions={0} | all-to-all | bytes 10485760 | tf_op jit(solution)/shard_map/all_to_all | solution.py:178
  (169 shorter events, 64.7 us)
Async XLA Ops:
  5.2 7.5 %copy-start = (s32[2,256]{1,0:T(2,128)S(1)}, s32[2,256]{1,0:T(2,128)}, u32[]{:S(2)}) copy-start(s32[2,256]{1,0:T(2,128)} %param.14) | copy-start | bytes 6148
  5.2 7.5 %copy-start.4 = (s32[2,256]{1,0:T(2,128)S(1)}, s32[2,256]{1,0:T(2,128)}, u32[]{:S(2)}) copy-start(s32[2,256]{1,0:T(2,128)} %param.19) | copy-start | bytes 6148
  5.2 7.5 %copy-start.5 = (s32[2,256]{1,0:T(2,128)S(1)}, s32[2,256]{1,0:T(2,128)}, u32[]{:S(2)}) copy-start(s32[2,256]{1,0:T(2,128)} %param.15) | copy-start | bytes 6148
  5.2 12.4 %all-to-all-start = ((bf16[40,2,32768]{2,0,1:T(8,128)(2,1)}), bf16[40,2,32768]{2,0,1:T(8,128)(2,1)}, u32[]{:S(2)}, u32[]{:S(2)}) async-start(bf16[40,2,32768]{2,0,1:T(8,128)(2,1)} %bitcast.87), calls=%async_computation | async-start | bytes 10485760 | tf_op jit(solution)/shard_map/all_to_all | solution.py:136
  17.6 27.1 %copy-start.1 = (f32[2,256]{1,0:T(2,128)S(1)}, f32[2,256]{1,0:T(2,128)}, u32[]{:S(2)}) copy-start(f32[2,256]{1,0:T(2,128)} %param.18) | copy-start | bytes 6148
  17.6 59.2 %copy-start.2 = (f32[2,256]{1,0:T(2,128)S(1)}, f32[2,256]{1,0:T(2,128)}, u32[]{:S(2)}) copy-start(f32[2,256]{1,0:T(2,128)} %param.16) | copy-start | bytes 6148
  17.6 59.2 %copy-start.3 = (f32[2,256]{1,0:T(2,128)S(1)}, f32[2,256]{1,0:T(2,128)}, u32[]{:S(2)}) copy-start(f32[2,256]{1,0:T(2,128)} %param.17) | copy-start | bytes 6148
  33.4 20.0 %all-to-all-start.1 = ((f32[64,2,160]{2,1,0:T(2,128)}), f32[64,2,160]{2,1,0:T(2,128)S(1)}, u32[]{:S(2)}, u32[]{:S(2)}) async-start(f32[64,2,160]{2,1,0:T(2,128)} %copy.33), calls=%async_computation.1 | async-start | bytes 262144 | tf_op jit(solution)/shard_map/all_to_all | solution.py:23
  63.1 13.4 %all-to-all-start.4 = ((f32[64,2,160]{2,1,0:T(2,128)}), f32[64,2,160]{2,1,0:T(2,128)S(1)}, u32[]{:S(2)}, u32[]{:S(2)}) async-start(f32[64,2,160]{2,1,0:T(2,128)} %broadcast_in_dim.96), calls=%async_computation.4 | async-start | bytes 262144 | tf_op jit(solution)/shard_map/all_to_all | solution.py:42
  150.1 13.4 %all-to-all-start.8 = ((f32[64,2,160]{2,1,0:T(2,128)}), f32[64,2,160]{2,1,0:T(2,128)S(1)}, u32[]{:S(2)}, u32[]{:S(2)}) async-start(f32[64,2,160]{2,1,0:T(2,128)} %broadcast_in_dim.101), calls=%async_computation.8 | async-start | bytes 262144 | tf_op jit(solution)/shard_map/all_to_all | solution.py:42
where the time goes:
time: 213 us; the launch traced here: 211 us
  matrix products  46.8 us (22%)
  blocking collectives  43.1 us (20%)
  local copies, waits for them, and re-layouts  40.2 us (19%)
  waiting for transfers between devices  30.8 us (14%)
  starting transfers between devices  28.3 us (13%)
  other arithmetic  21.1 us (10%)
    dot_general x16, matrix products, update_block(): lax.dot_general(increment, gain_matrix, (((1,), (1,)), ((), ())), preferr...  46.8 us
    reduce_sum x16, other arithmetic, update_block(): centred = (values - jnp.mean(values, axis=0)).astype(jnp.bfloat16)  19.4 us
    all_to_all x2, waiting for transfers between devices, sent_to_all(): lax.all_to_all(jnp.broadcast_to(array[None], (size, *array.shape)), axis,...  17.3 us
    all_to_all x2, local copies, waits for them, and re-layouts, on_device(): lax.all_to_all(background_ensemble, 'mem', split_axis=1, concat_axis=0, t...  14.7 us
    all_to_all x1, blocking collectives, sum_at_owner(): lax.all_to_all(blocks, axis, split_axis=0, concat_axis=0, tiled=True)  13.5 us
    all_to_all x2, blocking collectives, summed_rows(): return jnp.sum(lax.all_to_all(own, far, 0, 0, tiled=True), axis=0)  11.4 us
    all_to_all x1, starting transfers between devices, sum_at_owner(): lax.all_to_all(blocks, axis, split_axis=0, concat_axis=0, tiled=True)  11.2 us
    all_to_all x1, blocking collectives, on_device(): lax.all_to_all(realization_vectors, 'mem', split_axis=0, concat_axis=1, t...  10.8 us
  transfers between devices with their start and end apart: 4, of which 4 were waited for; matrix products, arithmetic and copies ran while one was open for 0% of the time, Pallas kernels for 0%

commit v1 on v0

--- a/solution.py
+++ b/solution.py
@@ -3,6 +3,7 @@
 from jax import lax
 from jax.sharding import Mesh
 from jax.sharding import PartitionSpec as P
+from jax.lax import all_to_all, psum
 
 ENSEMBLE_COUNT = 80
 SD = 32768
@@ -175,7 +176,12 @@
             anomaly,
             scaling,
         )
-    return lax.all_to_all(realization_vectors, "mem", split_axis=0, concat_axis=1, tiled=True)
+    return jnp.concatenate(
+        all_to_all(
+            jnp.stack(jnp.split(realization_vectors, psum(1, "mem"), 0), axis=0), "mem", 0, 0
+        ),
+        1,
+    )
 
 
 def solution(mesh):

time: 213 us -> 215 us (level)
  local copies, waits for them, and re-layouts: 40.2 us -> 43.1 us
    another operation x0 -> x1, local copies, waits for them, and re-layouts: none -> 2.87 us  [on_device(): jnp.stack(jnp.split(realization_vectors, psum(1, 'mem'), 0), axis=0)]
    all_to_all x1 -> x0, local copies, waits for them, and re-layouts: 2.73 us -> none  [on_device(): lax.all_to_all(realization_vectors, 'mem', split_axis=0, concat_axis=1, t...]
    reshape x0 -> x1, local copies, waits for them, and re-layouts: none -> 2.73 us  [on_device(): jnp.concatenate(all_to_all(jnp.stack(jnp.split(realization_vectors, psum(...]
where the time goes in v1:
time: 215 us; the launch traced here: 213 us
  matrix products  46.8 us (22%)
  local copies, waits for them, and re-layouts  43.1 us (20%)
  blocking collectives  41.7 us (19%)
  waiting for transfers between devices  30.8 us (14%)
  starting transfers between devices  28.3 us (13%)
  other arithmetic  21.6 us (10%)
    dot_general x16, matrix products, update_block(): lax.dot_general(increment, gain_matrix, (((1,), (1,)), ((), ())), preferr...  46.8 us
    reduce_sum x16, other arithmetic, update_block(): centred = (values - jnp.mean(values, axis=0)).astype(jnp.bfloat16)  19.4 us
    all_to_all x2, waiting for transfers between devices, sent_to_all(): lax.all_to_all(jnp.broadcast_to(array[None], (size, *array.shape)), axis,...  17.3 us
    all_to_all x2, local copies, waits for them, and re-layouts, on_device(): lax.all_to_all(background_ensemble, 'mem', split_axis=1, concat_axis=0, t...  14.7 us
    all_to_all x1, blocking collectives, sum_at_owner(): lax.all_to_all(blocks, axis, split_axis=0, concat_axis=0, tiled=True)  13.5 us
    all_to_all x2, blocking collectives, summed_rows(): return jnp.sum(lax.all_to_all(own, far, 0, 0, tiled=True), axis=0)  11.4 us
    all_to_all x1, starting transfers between devices, sum_at_owner(): lax.all_to_all(blocks, axis, split_axis=0, concat_axis=0, tiled=True)  11.2 us
    gather x2, local copies, waits for them, and re-layouts, collect_prior(): jnp.take(realization_vectors, col_offset + local_row, axis=1)  10.4 us
  transfers between devices with their start and end apart: 4, of which 4 were waited for; matrix products, arithmetic and copies ran while one was open for 0% of the time, Pallas kernels for 0%

profile of v1, /device:TPU:1, one launch (start us, length us, event | category | flops | bytes accessed | tf_op | source)
XLA Modules:
  0.0 213.0 jit_solution(3641703116043703978)
XLA Ops:
  0.0 5.2 %copy.48 = bf16[5,2,8,32768]{3,2,0,1:T(8,128)(2,1)} copy(bf16[5,2,8,32768]{3,2,1,0:T(8,128)(2,1)} %bitcast.92) | data formatting | bytes 10485760 | tf_op jit(solution)/shard_map/all_to_all | solution.py:137
  5.2 7.5 %all-to-all-start = ((bf16[40,2,32768]{2,0,1:T(8,128)(2,1)}), bf16[40,2,32768]{2,0,1:T(8,128)(2,1)}, u32[]{:S(2)}, u32[]{:S(2)}) async-start(bf16[40,2,32768]{2,0,1:T(8,128)(2,1)} %bitcast.90), calls=%async_computation | async-start | bytes 10485760 | tf_op jit(solution)/shard_map/all_to_all | solution.py:137
  12.8 4.8 %all-to-all-done = bf16[40,2,32768]{2,0,1:T(8,128)(2,1)} async-done(((bf16[40,2,32768]{2,0,1:T(8,128)(2,1)}), bf16[40,2,32768]{2,0,1:T(8,128)(2,1)}, u32[]{:S(2)}, u32[]{:S(2)}) %all-to-all-start) | async-done | bytes 5242912 | tf_op jit(solution)/shard_map/all_to_all | solution.py:137
  17.6 9.5 %copy.32 = bf16[80,32768]{0,1:T(8,128)(2,1)} copy(bf16[80,32768]{1,0:T(8,128)(2,1)} %bitcast.9) | data formatting | bytes 10485760 | tf_op jit(solution)/shard_map/all_to_all | solution.py:137
  27.2 5.2 %gather_fusion = bf16[256,80]{1,0:T(8,128)(2,1)S(1)} fusion(bf16[80,32768]{0,1:T(8,128)(2,1)} %copy.32, s32[1024]{0:T(1024)S(1)} %pad_clamp_fusion.1), kind=kCustom, calls=%fused_computation.clone | custom fusion | bytes 82944 | tf_op jit(solution)/shard_map/jit(_take)/gather | solution.py:104
  33.4 11.2 %all-to-all-start.1 = ((f32[64,2,160]{2,1,0:T(2,128)}), f32[64,2,160]{2,1,0:T(2,128)S(1)}, u32[]{:S(2)}, u32[]{:S(2)}) async-start(f32[64,2,160]{2,1,0:T(2,128)} %copy.34), calls=%async_computation.1 | async-start | bytes 262144 | tf_op jit(solution)/shard_map/all_to_all | solution.py:24
  44.7 8.7 %all-to-all-done.1 = f32[64,2,160]{2,1,0:T(2,128)S(1)} async-done(((f32[64,2,160]{2,1,0:T(2,128)}), f32[64,2,160]{2,1,0:T(2,128)S(1)}, u32[]{:S(2)}, u32[]{:S(2)}) %all-to-all-start.1) | async-done | bytes 81952 | tf_op jit(solution)/shard_map/all_to_all | solution.py:24
  53.5 5.2 %all_to_all.74 = f32[2,1,160]{2,1,0:T(1,128)S(1)} all-to-all(f32[2,1,160]{2,1,0:T(1,128)S(1)} %all_to_all.54), channel_id=1, replica_groups=mesh['mem'=2,'state_0'=4,'state_1'=4,'state_2'=4] {'mem'}, dimensions={0} | all-to-all | bytes 2560 | tf_op jit(solution)/shard_map/all_to_all | solution.py:31
  58.7 3.7 %all_to_all.75 = f32[2,1,160]{2,1,0:T(1,128)S(1)} all-to-all(f32[2,1,160]{2,1,0:T(1,128)S(1)} %broadcast_in_dim.94), channel_id=1, replica_groups=mesh['mem'=2,'state_0'=4,'state_1'=4,'state_2'=4] {'mem'}, dimensions={0} | all-to-all | bytes 2560 | tf_op jit(solution)/shard_map/all_to_all | solution.py:43
  63.1 4.7 %all-to-all-start.4 = ((f32[64,2,160]{2,1,0:T(2,128)}), f32[64,2,160]{2,1,0:T(2,128)S(1)}, u32[]{:S(2)}, u32[]{:S(2)}) async-start(f32[64,2,160]{2,1,0:T(2,128)} %broadcast_in_dim.96), calls=%async_computation.4 | async-start | bytes 262144 | tf_op jit(solution)/shard_map/all_to_all | solution.py:43
  67.8 8.7 %all-to-all-done.4 = f32[64,2,160]{2,1,0:T(2,128)S(1)} async-done(((f32[64,2,160]{2,1,0:T(2,128)}), f32[64,2,160]{2,1,0:T(2,128)S(1)}, u32[]{:S(2)}, u32[]{:S(2)}) %all-to-all-start.4) | async-done | bytes 81952 | tf_op jit(solution)/shard_map/all_to_all | solution.py:43
  76.9 33.8 %while.32 = (s32[]{:T(128)}, bf16[80,32768]{1,0:T(8,128)(2,1)}, f32[1,256]{1,0:T(1,128)S(1)}, s32[]{:T(128)}, s32[1,256]{1,0:T(1,128)S(1)}, /*index=5*/s32[256]{...) while((s32[]{:T(128)}, bf16[80,32768]{1,0:T(8,128)(2,1)}, ...), condition=%wide.region_6.8_spmd, body=%wide.region_4.7_spmd.sunk | while | flops 348720640 | bytes 3467987 | solution.py:121
  90.9 2.9 %fusion.48 = bf16[80,32768]{1,0:T(8,128)(2,1)} fusion(bf16[80,32768]{1,0:T(8,128)(2,1)} %get-tuple-element.803, s32[]{:T(128)S(6)} %select_n.138, bf16[80,256]{1,0:T(8,128)(2,1)S(1)} %get-tuple-element.827, bf16[80,4096]{1,0:T(8,128)(2,1)S(1)} %get-tuple-element.772, bf16[80,256]{1,0:T(8,128)(2,1)S(1)} %get-tuple-element.825, ...), kind=kOutput, calls=%fused_computation.8.clone.1 | convolution fusion | flops 347996160 | bytes 2084868 | tf_op jit(solution)/shard_map/while/body/eval_jaxpr/dot_general | solution.py:97
  110.6 9.5 %copy.36 = bf16[80,32768]{0,1:T(8,128)(2,1)} copy(bf16[80,32768]{1,0:T(8,128)(2,1)} %get-tuple-element.833) | data formatting | bytes 10485760 | tf_op jit(solution)/shard_map/while | solution.py:121
  120.1 5.2 %gather_fusion.1 = bf16[256,80]{1,0:T(8,128)(2,1)S(1)} fusion(bf16[80,32768]{0,1:T(8,128)(2,1)} %copy.36, s32[1024]{0:T(1024)S(1)} %pad_clamp_fusion), kind=kCustom, calls=%fused_computation.1.clone | custom fusion | bytes 82944 | tf_op jit(solution)/shard_map/jit(_take)/gather | solution.py:104
  125.8 13.5 %all_to_all.76 = f32[64,2,160]{2,1,0:T(2,128)S(1)} all-to-all(f32[64,2,160]{2,1,0:T(2,128)S(1)} %copy.38), channel_id=1, replica_groups=mesh['mem'=2,'state_0'=4,'state_1'=4,'state_2'=4] {'state_0','state_1','..., dimensions={0} | all-to-all | bytes 163840 | tf_op jit(solution)/shard_map/all_to_all | solution.py:24
  139.4 6.2 %all_to_all.77 = f32[2,1,160]{2,1,0:T(1,128)S(1)} all-to-all(f32[2,1,160]{2,1,0:T(1,128)S(1)} %all_to_all.59), channel_id=1, replica_groups=mesh['mem'=2,'state_0'=4,'state_1'=4,'state_2'=4] {'mem'}, dimensions={0} | all-to-all | bytes 2560 | tf_op jit(solution)/shard_map/all_to_all | solution.py:31
  145.7 3.7 %all_to_all.78 = f32[2,1,160]{2,1,0:T(1,128)S(1)} all-to-all(f32[2,1,160]{2,1,0:T(1,128)S(1)} %broadcast_in_dim.99), channel_id=1, replica_groups=mesh['mem'=2,'state_0'=4,'state_1'=4,'state_2'=4] {'mem'}, dimensions={0} | all-to-all | bytes 2560 | tf_op jit(solution)/shard_map/all_to_all | solution.py:43
  150.1 4.9 %all-to-all-start.8 = ((f32[64,2,160]{2,1,0:T(2,128)}), f32[64,2,160]{2,1,0:T(2,128)S(1)}, u32[]{:S(2)}, u32[]{:S(2)}) async-start(f32[64,2,160]{2,1,0:T(2,128)} %broadcast_in_dim.101), calls=%async_computation.8 | async-start | bytes 262144 | tf_op jit(solution)/shard_map/all_to_all | solution.py:43
  154.9 8.6 %all-to-all-done.8 = f32[64,2,160]{2,1,0:T(2,128)S(1)} async-done(((f32[64,2,160]{2,1,0:T(2,128)}), f32[64,2,160]{2,1,0:T(2,128)S(1)}, u32[]{:S(2)}, u32[]{:S(2)}) %all-to-all-start.8) | async-done | bytes 81952 | tf_op jit(solution)/shard_map/all_to_all | solution.py:43
  163.8 33.8 %while.33 = (s32[]{:T(128)}, bf16[80,32768]{1,0:T(8,128)(2,1)}, f32[1,256]{1,0:T(1,128)S(1)}, s32[]{:T(128)}, s32[1,256]{1,0:T(1,128)S(1)}, /*index=5*/s32[256]{...) while((s32[]{:T(128)}, bf16[80,32768]{1,0:T(8,128)(2,1)}, ...), condition=%wide.region_13.15_spmd, body=%wide.region_11.14_spmd.sunk | while | flops 348720640 | bytes 3467987 | solution.py:121
  177.8 3.0 %fusion.52 = bf16[80,32768]{1,0:T(8,128)(2,1)} fusion(bf16[80,32768]{1,0:T(8,128)(2,1)} %get-tuple-element.848, s32[]{:T(128)S(6)} %select_n.141, bf16[80,256]{1,0:T(8,128)(2,1)S(1)} %get-tuple-element.872, bf16[80,4096]{1,0:T(8,128)(2,1)S(1)} %get-tuple-element.785, bf16[80,256]{1,0:T(8,128)(2,1)S(1)} %get-tuple-element.870, ...), kind=kOutput, calls=%fused_computation.38.clone.1 | convolution fusion | flops 347996160 | bytes 2084868 | tf_op jit(solution)/shard_map/while/body/eval_jaxpr/dot_general | solution.py:97
  194.7 2.9 %fusion.52 = bf16[80,32768]{1,0:T(8,128)(2,1)} fusion(bf16[80,32768]{1,0:T(8,128)(2,1)} %get-tuple-element.848, s32[]{:T(128)S(6)} %select_n.141, bf16[80,256]{1,0:T(8,128)(2,1)S(1)} %get-tuple-element.872, bf16[80,4096]{1,0:T(8,128)(2,1)S(1)} %get-tuple-element.785, bf16[80,256]{1,0:T(8,128)(2,1)S(1)} %get-tuple-element.870, ...), kind=kOutput, calls=%fused_computation.38.clone.1 | convolution fusion | flops 347996160 | bytes 2084868 | tf_op jit(solution)/shard_map/while/body/eval_jaxpr/dot_general | solution.py:97
  200.9 9.3 %all_to_all.79 = bf16[2,40,32768]{2,1,0:T(8,128)(2,1)S(1)} all-to-all(bf16[2,40,32768]{2,1,0:T(8,128)(2,1)S(1)} %pad_maximum_fusion), channel_id=1, replica_groups=mesh['mem'=2,'state_0'=4,'state_1'=4,'state_2'=4] {'mem'}, dimensions={0} | all-to-all | bytes 10485760 | tf_op jit(solution)/shard_map/all_to_all | solution.py:180
  (171 shorter events, 68.0 us)
Async XLA Ops:
  5.2 7.5 %copy-start = (s32[2,256]{1,0:T(2,128)S(1)}, s32[2,256]{1,0:T(2,128)}, u32[]{:S(2)}) copy-start(s32[2,256]{1,0:T(2,128)} %param.14) | copy-start | bytes 6148
  5.2 7.5 %copy-start.4 = (s32[2,256]{1,0:T(2,128)S(1)}, s32[2,256]{1,0:T(2,128)}, u32[]{:S(2)}) copy-start(s32[2,256]{1,0:T(2,128)} %param.19) | copy-start | bytes 6148
  5.2 7.5 %copy-start.5 = (s32[2,256]{1,0:T(2,128)S(1)}, s32[2,256]{1,0:T(2,128)}, u32[]{:S(2)}) copy-start(s32[2,256]{1,0:T(2,128)} %param.15) | copy-start | bytes 6148
  5.2 12.4 %all-to-all-start = ((bf16[40,2,32768]{2,0,1:T(8,128)(2,1)}), bf16[40,2,32768]{2,0,1:T(8,128)(2,1)}, u32[]{:S(2)}, u32[]{:S(2)}) async-start(bf16[40,2,32768]{2,0,1:T(8,128)(2,1)} %bitcast.90), calls=%async_computation | async-start | bytes 10485760 | tf_op jit(solution)/shard_map/all_to_all | solution.py:137
  17.6 27.1 %copy-start.1 = (f32[2,256]{1,0:T(2,128)S(1)}, f32[2,256]{1,0:T(2,128)}, u32[]{:S(2)}) copy-start(f32[2,256]{1,0:T(2,128)} %param.18) | copy-start | bytes 6148
  17.6 59.2 %copy-start.2 = (f32[2,256]{1,0:T(2,128)S(1)}, f32[2,256]{1,0:T(2,128)}, u32[]{:S(2)}) copy-start(f32[2,256]{1,0:T(2,128)} %param.16) | copy-start | bytes 6148
  17.6 59.2 %copy-start.3 = (f32[2,256]{1,0:T(2,128)S(1)}, f32[2,256]{1,0:T(2,128)}, u32[]{:S(2)}) copy-start(f32[2,256]{1,0:T(2,128)} %param.17) | copy-start | bytes 6148
  33.4 20.0 %all-to-all-start.1 = ((f32[64,2,160]{2,1,0:T(2,128)}), f32[64,2,160]{2,1,0:T(2,128)S(1)}, u32[]{:S(2)}, u32[]{:S(2)}) async-start(f32[64,2,160]{2,1,0:T(2,128)} %copy.34), calls=%async_computation.1 | async-start | bytes 262144 | tf_op jit(solution)/shard_map/all_to_all | solution.py:24
  63.1 13.4 %all-to-all-start.4 = ((f32[64,2,160]{2,1,0:T(2,128)}), f32[64,2,160]{2,1,0:T(2,128)S(1)}, u32[]{:S(2)}, u32[]{:S(2)}) async-start(f32[64,2,160]{2,1,0:T(2,128)} %broadcast_in_dim.96), calls=%async_computation.4 | async-start | bytes 262144 | tf_op jit(solution)/shard_map/all_to_all | solution.py:43
  150.1 13.4 %all-to-all-start.8 = ((f32[64,2,160]{2,1,0:T(2,128)}), f32[64,2,160]{2,1,0:T(2,128)S(1)}, u32[]{:S(2)}, u32[]{:S(2)}) async-start(f32[64,2,160]{2,1,0:T(2,128)} %broadcast_in_dim.101), calls=%async_computation.8 | async-start | bytes 262144 | tf_op jit(solution)/shard_map/all_to_all | solution.py:43
